TPU v7x, 32 devices: a whole 2x2x4 slice. The times are simulated.
32 devices in a mesh: seq: 16 (over z, x, core), head: 2 (over y).
Axes of the slice: x: 2, y: 2, z: 4, core: 2. Of those that a mesh axis runs over, the one named last changes fastest.
Arguments:
- qkv: bfloat16 [3, 8192, 4096], P(None, ('seq', 'head')), may hold values from -6 to 6
- send_rows: int32 [16, 16, 40], P('seq'), may hold values from -1 to 511, as said below
- recv_pos: int32 [16, 16, 40], P('seq'), may hold values from -1 to 511, as said below
- req_lengths: int32 [4], replicated, may hold values from 1 to 4096, 8192 in all
- norm_gain: float32 [4096], P('head'), may hold values from 0.5 to 1.5
Outputs:
- attn_out: bfloat16 [8192, 4096], P('seq', 'head')
Inputs may be any that keep to these rules, and one draw needn't show every extreme that they name: send_rows[l, o, c] is a row of loader group l (rows l * 512 to l * 512 + 511 of qkv, counted from the group's first) sent to owner o in slot c, or -1 for an empty slot; used slots come first. Every row of a group is sent exactly once. At most 40 rows go from one group to one owner, and in every draw some pairs carry exactly 40, so that every group sends and every owner receives 40 rows from one pair. The number of rows from group l to owner o depends only on (o - l) modulo the number of groups. recv_pos[o, l, c] is the position within owner o's block of 512 packed positions where slot c from group l lands, and -1 exactly where send_rows[l, o, c] is -1; every position of a block is filled exactly once.
All inputs are finite; a program needn't handle non-finite values.
Results may differ from a plain program's by a relative error of at most 0.003.
Values may be sent and summed in bfloat16 or wider, within the bound.
No kernel may reach another device: no remote copies, remote signals or barrier semaphores. Data moves between devices by JAX's collectives and lax.ppermute only.
A program may use at most 128 MiB of HBM per device.

v0:
```python
import jax
import jax.numpy as jnp
from jax import lax
from jax.sharding import PartitionSpec as P

HEAD_DIM = 128
norm_eps = 1e-06


def prefix(shard, axis, combine, identity):
    length, position = (lax.axis_size(axis), lax.axis_index(axis))
    everything = jax.tree.map(lambda part: lax.all_gather(part, axis), shard)
    start = jax.tree.map(
        lambda part, zero: jnp.broadcast_to(jnp.asarray(zero, part.dtype), part.shape),
        shard,
        identity,
    )

    def lap(k, before):
        reached = k < position
        new = combine(before, jax.tree.map(lambda part: part[k], everything))
        return jax.tree.map(lambda a, b: jnp.where(reached, a, b), new, before)

    return lax.fori_loop(0, length, lap, start)


def place_rows(incoming, land_rows, tok_rows):
    row_width = incoming.shape[-1]
    planes = incoming.shape[0]
    flat_rows = incoming.reshape(planes, -1, row_width)
    land_index = jnp.where(land_rows < 0, tok_rows, land_rows).reshape(-1)
    blank_rows = jnp.zeros((planes, tok_rows, row_width), incoming.dtype)
    return blank_rows.at[:, land_index].set(flat_rows, mode="drop")


def carry_combine(earlier, later):
    return (later[0] + (1.0 - later[1]) * earlier[0], jnp.maximum(earlier[1], later[1]))


def on_device(qkv, send_rows, recv_pos, req_lengths, norm_gain):
    seq_count = lax.axis_size("seq")
    slot_count = send_rows.shape[2]
    pick_rows = jnp.maximum(send_rows[0], 0).reshape(-1)
    land_rows = recv_pos[0]
    grouped = lax.all_to_all(qkv, "head", split_axis=2, concat_axis=1, tiled=True)
    outgoing = jnp.take(grouped, pick_rows, axis=1).reshape(
        3, seq_count, slot_count, grouped.shape[2]
    )
    arrived = lax.all_to_all(outgoing, "seq", split_axis=1, concat_axis=1, tiled=True)
    packed = place_rows(arrived, land_rows, grouped.shape[1])
    query, keys, values = (packed[0], packed[1], packed[2])
    tok_rows = keys.shape[0]
    head_count = keys.shape[1] // HEAD_DIM
    first_row = lax.axis_index("seq") * tok_rows
    req_ends = jnp.cumsum(req_lengths)
    req_starts = req_ends - req_lengths
    positions = first_row + jnp.arange(tok_rows, dtype=jnp.int32)
    segment = jnp.sum((req_starts[None, :] <= positions[:, None]).astype(jnp.int32), axis=1) - 1
    prev_segment = jnp.sum((req_starts < first_row).astype(jnp.int32)) - 1
    inside = jnp.any((req_starts >= first_row) & (req_starts < first_row + tok_rows))
    has_start = jnp.where(inside, 1.0, 0.0).astype(jnp.float32)
    carried_mask = segment == prev_segment
    tail_mask = segment == segment[tok_rows - 1]
    causal = (positions[None, :] <= positions[:, None]) & (segment[None, :] == segment[:, None])
    tail_keys = jnp.where(tail_mask[:, None], keys, jnp.zeros_like(keys))
    update = jnp.einsum(
        "shd,she->hde",
        tail_keys.reshape(tok_rows, head_count, HEAD_DIM),
        values.reshape(tok_rows, head_count, HEAD_DIM),
        preferred_element_type=jnp.float32,
    )
    identity = (jnp.zeros_like(update), jnp.zeros((), jnp.float32))
    carried_pair = prefix((update, has_start), "seq", carry_combine, identity)
    carried = carried_pair[0]
    outputs = []
    for number in range(head_count):
        columns = slice(number * HEAD_DIM, (number + 1) * HEAD_DIM)
        query_head = query[:, columns]
        key_head = keys[:, columns]
        value_head = values[:, columns]
        scores = lax.dot_general(
            query_head, key_head, (((1,), (1,)), ((), ())), preferred_element_type=jnp.float32
        )
        weights = jnp.where(causal, scores, 0.0).astype(jnp.bfloat16)
        local_term = jnp.dot(weights, value_head, preferred_element_type=jnp.float32)
        carried_term = jnp.dot(
            query_head.astype(jnp.float32),
            carried[number],
            precision=lax.Precision.HIGHEST,
            preferred_element_type=jnp.float32,
        )
        raw_out = local_term + jnp.where(carried_mask[:, None], carried_term, 0.0)
        inv_rms = lax.rsqrt(jnp.mean(raw_out * raw_out, axis=1, keepdims=True) + norm_eps)
        outputs.append((raw_out * inv_rms * norm_gain[columns][None, :]).astype(jnp.bfloat16))
    return jnp.concatenate(outputs, axis=1)


def solution(mesh):
    return jax.shard_map(
        on_device,
        mesh=mesh,
        in_specs=(
            P(None, ("seq", "head"), None),
            P("seq", None, None),
            P("seq", None, None),
            P(),
            P("head"),
        ),
        out_specs=P("seq", "head"),
        check_vma=False,
    )
```

profile of v0, /device:TPU:0, one launch (start us, length us, event | category | flops | bytes accessed | tf_op | source)
XLA Modules:
  0.0 782.3 jit_solution(8094631923778563405)
XLA Ops:
  6.5 13.1 %copy.40 = bf16[3,256,4096]{1,0,2:T(4,128)(2,1)} copy(bf16[3,256,4096]{2,1,0:T(8,128)(2,1)} %param.7) | data formatting | bytes 12582912 | tf_op args[0]
  19.6 7.1 all-to-all-start
  26.8 93.7 %all-to-all-done = bf16[3,256,4096]{1,0,2:T(4,128)(2,1)} async-done(((bf16[3,256,4096]{1,0,2:T(4,128)(2,1)}), bf16[3,256,4096]{1,0,2:T(4,128)(2,1)}, u32[]{:S(2)}, u32[]{:S(2)}) %all-to-all-start) | async-done | bytes 6291488 | tf_op jit(solution)/shard_map/all_to_all | solution.py:45
  120.6 7.0 copy.41
  127.5 8.7 %copy.42 = bf16[3,2,256,2048]{3,2,1,0:T(8,128)(2,1)} copy(bf16[3,2,256,2048]{2,3,1,0:T(8,128)(2,1)} %bitcast.90) | data formatting | bytes 12582912 | tf_op jit(solution)/shard_map/all_to_all | solution.py:45
  136.2 11.5 %copy.43 = bf16[3,512,2048]{2,0,1:T(4,128)(2,1)} copy(bf16[3,512,2048]{2,1,0:T(8,128)(2,1)} %bitcast.91) | data formatting | bytes 12582912 | tf_op jit(solution)/shard_map/all_to_all | solution.py:45
  147.7 24.7 %gather_fusion = bf16[640,3,2048]{2,1,0:T(4,128)(2,1)} fusion(bf16[3,512,2048]{2,0,1:T(4,128)(2,1)} %copy.43, s32[1024]{0:T(1024)S(1)} %pad_clamp_fusion), kind=kCustom, calls=%fused_computation | custom fusion | bytes 15731200 | tf_op jit(solution)/shard_map/jit(_take)/gather | solution.py:46
  172.5 16.3 %copy_select_fusion = bf16[3,16,40,2048]{3,2,0,1:T(8,128)(2,1)} fusion(bf16[3,16,40,2048]{3,0,2,1:T(4,128)(2,1)} %bitcast.88, pred[16,40]{1,0:T(8,128)(4,1)S(1)} %compare_bitcast_fusion), kind=kLoop, calls=%fused_computation.4 | loop fusion | flops 3932160 | bytes 15729280 | tf_op jit(solution)/shard_map/jit(_take)/select_n | solution.py:46
  188.7 6.2 all-to-all-start.1
  198.7 137.9 %all-to-all-done.1 = bf16[3,16,40,2048]{3,2,0,1:T(8,128)(2,1)} async-done(((bf16[3,16,40,2048]{3,2,0,1:T(8,128)(2,1)}), bf16[3,16,40,2048]{3,2,0,1:T(8,128)(2,1)}, u32[]{:S(2)}, u32[]{:S(2)}) %all-to-all-start.1) | async-done | bytes 7864352 | tf_op jit(solution)/shard_map/all_to_all | solution.py:49
  336.6 4.2 copy.45
  340.8 25.5 %copy.46 = bf16[640,3,2048]{2,1,0:T(4,128)(2,1)} copy(bf16[640,3,2048]{2,0,1:T(8,128)(2,1)S(1)} %bitcast.89) | data formatting | bytes 15728640 | tf_op jit(solution)/shard_map/reshape | solution.py:30
  366.3 7.6 broadcast_in_dim.178
  373.9 85.0 %scatter_fusion = bf16[3,512,2048]{2,0,1:T(4,128)(2,1)} fusion(bf16[3,512,2048]{2,0,1:T(4,128)(2,1)} %broadcast_in_dim.178, s32[640]{0:T(1024)S(1)} %fusion.213, bf16[640,3,2048]{2,1,0:T(4,128)(2,1)} %copy.46), kind=kCustom, calls=%fused_computation.1 | custom fusion | bytes 23595520 | tf_op jit(solution)/shard_map/scatter | solution.py:33
  459.0 20.8 %fusion.232 = (bf16[1,512,2048]{2,0,1:T(2,128)(2,1)}, bf16[1,512,2048]{2,0,1:T(2,128)(2,1)}, bf16[1,512,2048]{2,0,1:T(2,128)(2,1)}) fusion(bf16[3,512,2048]{2,0,1:T(4,128)(2,1)} %scatter_fusion), kind=kLoop, calls=%fused_computation.301 | loop fusion | bytes 12582912 | tf_op jit(solution)/shard_map/slice | solution.py:51
  479.8 9.0 %copy.47 = bf16[1,512,2048]{1,2,0:T(8,128)(2,1)S(1)} copy(bf16[1,512,2048]{2,0,1:T(2,128)(2,1)} %get-tuple-element.130) | data formatting | bytes 4194304 | tf_op jit(solution)/shard_map/slice | solution.py:51
  488.8 10.5 %copy.48 = bf16[1,512,2048]{1,2,0:T(8,128)(2,1)} copy(bf16[1,512,2048]{2,0,1:T(2,128)(2,1)} %get-tuple-element.131) | data formatting | bytes 4194304 | tf_op jit(solution)/shard_map/slice | solution.py:51
  499.3 3.3 fusion.1
  504.5 63.3 %all-reduce = f32[16]{0:T(128)S(1)} all-reduce(f32[16]{0:T(128)S(1)} %dynamic-update-slice), channel_id=1, replica_groups=mesh['seq'=16,'head'=2] {'seq'}, use_global_device_ids=true, to_apply=%add | all-reduce | flops 16 | bytes 128
  567.8 3.6 copy.59
  571.5 6.9 copy_bitcast_fusion
  578.4 80.6 %all-gather.3.cloned.1.call-done = f32[256,128,128]{2,1,0:T(8,128)} async-done(((f32[16,128,128]{2,1,0:T(8,128)}), f32[256,128,128]{2,1,0:T(8,128)}) %all-gather.3.cloned.1.call-update) | async-done | bytes 16777232 | tf_op jit(solution)/shard_map/all_gather | solution.py:12
  658.9 54.5 %while.14 = (s32[]{:T(128)}, f32[16,128,128]{2,1,0:T(8,128)S(1)}, s32[]{:T(128)}, f32[16,16,128,128]{3,2,1,0:T(8,128)}, f32[16]{0:T(128)S(1)}, /*index=5*/s32[]{:T(128)}, f32[1]{0:T(128)}, s32[]{:T(128)}) while((s32[]{:T(128)}, f32[16,128,128]{2,1,0:T(8,128)S(1)}, s32[]{:T(128)}, f32[16,16,128,128]{3,2,1,0:T(8,128)}, ...), condition=%wide.region_6.7_spmd.clone, body=%wide.region_5.6_spmd.clone.sunk | while | flops 1048581 | bytes 3145873 | solution.py:24
  731.6 2.4 multiply_reduce_fusion.4
  (177 shorter events, 107.3 us)
Async XLA Ops:
  19.6 7.1 copy-start.25
  19.6 100.9 %all-to-all-start = ((bf16[3,256,4096]{1,0,2:T(4,128)(2,1)}), bf16[3,256,4096]{1,0,2:T(4,128)(2,1)}, u32[]{:S(2)}, u32[]{:S(2)}) async-start(bf16[3,256,4096]{1,0,2:T(4,128)(2,1)} %copy.40), calls=%async_computation | async-start | bytes 16777216 | tf_op jit(solution)/shard_map/all_to_all | solution.py:45
  188.7 6.3 copy-start.28
  188.7 7.8 %copy-start.26 = (s32[1,16,40]{2,1,0:T(8,128)S(1)}, s32[1,16,40]{2,1,0:T(8,128)}, u32[]{:S(2)}) copy-start(s32[1,16,40]{2,1,0:T(8,128)} %param.9) | copy-start | bytes 7684
  188.7 147.8 %all-to-all-start.1 = ((bf16[3,16,40,2048]{3,2,0,1:T(8,128)(2,1)}), bf16[3,16,40,2048]{3,2,0,1:T(8,128)(2,1)}, u32[]{:S(2)}, u32[]{:S(2)}) async-start(bf16[3,16,40,2048]{3,2,0,1:T(8,128)(2,1)} %copy_select_fusion), calls=%async_computation.1 | async-start | bytes 15728640 | tf_op jit(solution)/shard_map/all_to_all | solution.py:49
  195.0 464.0 %all-gather.3.cloned.1.call-start = ((), (), s32[]{:S(2)}) async-start(), calls=%async_computation.2 | async-start | bytes 17825792 | tf_op jit(solution)/shard_map/all_gather | solution.py:12
  499.3 68.5 %copy-start.27 = (f32[2048]{0:T(1024)S(1)}, f32[2048]{0:T(1024)}, u32[]{:S(2)}) copy-start(f32[2048]{0:T(1024)} %param.11) | copy-start | bytes 24580
  731.6 4.7 copy-start.23
  738.6 4.6 copy-start.20
  740.9 4.6 copy-start.19
  743.2 4.6 copy-start.18
  745.5 4.6 copy-start.17
  747.8 4.6 copy-start.16
  750.1 4.6 copy-start.15
  752.4 4.6 copy-start.14
  754.7 4.6 copy-start.13
  757.0 4.6 copy-start.12
  766.0 5.5 copy-start.10
  766.1 5.6 copy-start.7
  766.1 5.7 copy-start.6
  766.1 5.8 copy-start.4
  766.1 5.9 copy-start.3
  766.1 6.0 copy-start.2
  767.3 5.0 copy-start.1
  (9 other events, 30.9 us)
Sparse Core Ops, SparseCore 0:
  502.7 156.1 all-gather.2
where the time goes:
time: 794 us; the launch traced here: 782 us
  waiting for transfers between devices  312 us (39%)
  local copies, waits for them, and re-layouts  253 us (32%)
  blocking collectives  63.3 us (8%)
  other arithmetic  59.2 us (7%)
  matrix products  55.6 us (7%)
  between operations  15.6 us (2%)
  starting transfers between devices  13.3 us (2%)
  loops' own time  10.4 us (1%)
    all_to_all x1, waiting for transfers between devices, on_device(): lax.all_to_all(outgoing, 'seq', split_axis=1, concat_axis=1, tiled=True)  138 us
    all_to_all x1, waiting for transfers between devices, on_device(): lax.all_to_all(qkv, 'head', split_axis=2, concat_axis=1, tiled=True)  93.7 us
    scatter x1, local copies, waits for them, and re-layouts, place_rows(): return blank_rows.at[:, land_index].set(flat_rows, mode='drop')  85 us
    all_gather x1, waiting for transfers between devices, prefix(): everything = jax.tree.map(lambda part: lax.all_gather(part, axis), shard)  80.6 us
    unnamed x1, blocking collectives  63.3 us
    slice x3, local copies, waits for them, and re-layouts, on_device(): query, keys, values = (packed[0], packed[1], packed[2])  40.3 us
    dot_general x16, matrix products, on_device(): jnp.dot(weights, value_head, preferred_element_type=jnp.float32)  35.8 us
    select_n x16, other arithmetic, lap(): return jax.tree.map(lambda a, b: jnp.where(reached, a, b), new, before)  34.2 us
  transfers between devices with their start and end apart: 3, of which 3 were waited for; matrix products, arithmetic and copies ran while one was open for 2% of the time, Pallas kernels for 0%

commit v1 on v0

--- a/solution.py
+++ b/solution.py
@@ -5,6 +5,17 @@
 
 HEAD_DIM = 128
 norm_eps = 1e-06
+
+
+def spread_stops_all(z_in, dim_at, my_data):
+    aux, e_now = (z_in.shape[:dim_at], z_in.shape[dim_at + 1 :])
+    return jnp.moveaxis(z_in.reshape(*aux, my_data, -1, *e_now), dim_at, 0)
+
+
+def see_ratios(slab_in, dimension_no):
+    tall = list(slab_in.shape[1:])
+    tall[dimension_no] *= slab_in.shape[0]
+    return jnp.moveaxis(slab_in, 0, dimension_no).reshape(tall)
 
 
 def prefix(shard, axis, combine, identity):
@@ -38,6 +49,19 @@
 
 
 def on_device(qkv, send_rows, recv_pos, req_lengths, norm_gain):
+
+    def save_islands_by_axis(matrix, dev_axis, obj, unit):
+        top, spare = (jax.lax.axis_size(dev_axis), jax.lax.axis_index(dev_axis))
+        carry_out = spread_stops_all(matrix, obj, top)
+        parts_seen = [carry_out[spare]]
+        for s in range(1, top):
+            ready = carry_out[(spare + s) % top]
+            parts_seen.append(
+                jax.lax.ppermute(ready, dev_axis, [(pp, (pp + s) % top) for pp in range(top)])
+            )
+        carry_out = jnp.stack(parts_seen, axis=0)[(spare - jnp.arange(top)) % top]
+        return see_ratios(carry_out, unit)
+
     seq_count = lax.axis_size("seq")
     slot_count = send_rows.shape[2]
     pick_rows = jnp.maximum(send_rows[0], 0).reshape(-1)
@@ -46,7 +70,7 @@
     outgoing = jnp.take(grouped, pick_rows, axis=1).reshape(
         3, seq_count, slot_count, grouped.shape[2]
     )
-    arrived = lax.all_to_all(outgoing, "seq", split_axis=1, concat_axis=1, tiled=True)
+    arrived = save_islands_by_axis(outgoing, "seq", 1, 1)
     packed = place_rows(arrived, land_rows, grouped.shape[1])
     query, keys, values = (packed[0], packed[1], packed[2])
     tok_rows = keys.shape[0]

time: 794 us -> 819 us (1.031)
  starting transfers between devices: 13.3 us -> 91.6 us
  waiting for transfers between devices: 312 us -> 250 us
  local copies, waits for them, and re-layouts: 253 us -> 297 us
  blocking collectives: 63.3 us -> 34.7 us
  other arithmetic: 59.2 us -> 50.6 us
    all_to_all x1 -> x0, waiting for transfers between devices: 138 us -> none  [on_device(): lax.all_to_all(outgoing, 'seq', split_axis=1, concat_axis=1, tiled=True)]
    ppermute x0 -> x15, starting transfers between devices: none -> 84.5 us  [save_islands_by_axis(): jax.lax.ppermute(ready, dev_axis, [(pp, (pp + s) % top) for pp in range(t...]
    ppermute x0 -> x15, waiting for transfers between devices: none -> 79.1 us  [save_islands_by_axis(): jax.lax.ppermute(ready, dev_axis, [(pp, (pp + s) % top) for pp in range(t...]
    another operation x0 -> x18, local copies, waits for them, and re-layouts: none -> 38.1 us  [the longest x1 25.3 us: place_rows(): flat_rows = incoming.reshape(planes, -1, row_width)]
    unnamed x1, blocking collectives: 63.3 us -> 34.7 us
    reshape x1 -> x0, local copies, waits for them, and re-layouts: 25.5 us -> none  [place_rows(): flat_rows = incoming.reshape(planes, -1, row_width)]
    gather x0 -> x1, local copies, waits for them, and re-layouts: none -> 18.2 us  [save_islands_by_axis(): carry_out = jnp.stack(parts_seen, axis=0)[(spare - jnp.arange(top)) % top]]
    unnamed x66 -> x81, local copies, waits for them, and re-layouts: 25 us -> 38 us
  transfers between devices with their start and end apart: 3 -> 17, of which waited for: 3 -> 7; matrix products, arithmetic and copies ran while one was open for 2% -> 4% of each run, Pallas kernels for 0% -> 0%
where the time goes in v1:
time: 819 us; the launch traced here: 807 us
  local copies, waits for them, and re-layouts  297 us (36%)
  waiting for transfers between devices  250 us (31%)
  starting transfers between devices  91.6 us (11%)
  matrix products  55.2 us (7%)
  other arithmetic  50.6 us (6%)
  blocking collectives  34.7 us (4%)
  between operations  16.1 us (2%)
  loops' own time  11.7 us (1%)
    all_to_all x1, waiting for transfers between devices, on_device(): lax.all_to_all(qkv, 'head', split_axis=2, concat_axis=1, tiled=True)  89.6 us
    scatter x1, local copies, waits for them, and re-layouts, place_rows(): return blank_rows.at[:, land_index].set(flat_rows, mode='drop')  85.1 us
    ppermute x15, starting transfers between devices, save_islands_by_axis(): jax.lax.ppermute(ready, dev_axis, [(pp, (pp + s) % top) for pp in range(t...  84.5 us
    all_gather x1, waiting for transfers between devices, prefix(): everything = jax.tree.map(lambda part: lax.all_gather(part, axis), shard)  81.7 us
    ppermute x15, waiting for transfers between devices, save_islands_by_axis(): jax.lax.ppermute(ready, dev_axis, [(pp, (pp + s) % top) for pp in range(t...  79.1 us
    slice x3, local copies, waits for them, and re-layouts, on_device(): query, keys, values = (packed[0], packed[1], packed[2])  40.2 us
    unnamed x81, local copies, waits for them, and re-layouts  38 us
    dot_general x16, matrix products, on_device(): jnp.dot(weights, value_head, preferred_element_type=jnp.float32)  35.7 us
  transfers between devices with their start and end apart: 17, of which 7 were waited for; matrix products, arithmetic and copies ran while one was open for 4% of the time, Pallas kernels for 0%

profile of v1, /device:TPU:0, one launch (start us, length us, event | category | flops | bytes accessed | tf_op | source)
XLA Modules:
  0.0 807.0 jit_solution(13320864263169126828)
XLA Ops:
  6.5 13.1 %copy.80 = bf16[3,256,4096]{1,0,2:T(4,128)(2,1)} copy(bf16[3,256,4096]{2,1,0:T(8,128)(2,1)} %param.7) | data formatting | bytes 12582912 | tf_op args[0]
  19.6 7.1 all-to-all-start
  30.9 89.6 %all-to-all-done = bf16[3,256,4096]{1,0,2:T(4,128)(2,1)} async-done(((bf16[3,256,4096]{1,0,2:T(4,128)(2,1)}), bf16[3,256,4096]{1,0,2:T(4,128)(2,1)}, u32[]{:S(2)}, u32[]{:S(2)}) %all-to-all-start) | async-done | bytes 6291488 | tf_op jit(solution)/shard_map/all_to_all | solution.py:69
  120.6 7.0 copy.81
  127.5 8.7 %copy.82 = bf16[3,2,256,2048]{3,2,1,0:T(8,128)(2,1)} copy(bf16[3,2,256,2048]{2,3,1,0:T(8,128)(2,1)} %bitcast.174) | data formatting | bytes 12582912 | tf_op jit(solution)/shard_map/all_to_all | solution.py:69
  136.2 11.5 %copy.83 = bf16[3,512,2048]{2,0,1:T(4,128)(2,1)} copy(bf16[3,512,2048]{2,1,0:T(8,128)(2,1)} %bitcast.175) | data formatting | bytes 12582912 | tf_op jit(solution)/shard_map/all_to_all | solution.py:69
  147.7 24.3 %gather_fusion = bf16[640,3,2048]{2,1,0:T(4,128)(2,1)} fusion(bf16[3,512,2048]{2,0,1:T(4,128)(2,1)} %copy.83, s32[1024]{0:T(1024)S(1)} %pad_clamp_fusion.1), kind=kCustom, calls=%fused_computation | custom fusion | bytes 15731200 | tf_op jit(solution)/shard_map/jit(_take)/gather | solution.py:70
  172.0 7.5 broadcast_select_fusion
  219.3 67.6 %collective-permute-done.4 = bf16[3,1,40,2048]{3,2,0,1:T(8,128)(2,1)S(1)} collective-permute-done((bf16[3,1,40,2048]{3,2,0,1:T(8,128)(2,1)S(1)}, bf16[3,1,40,2048]{3,2,0,1:T(8,128)(2,1)S(1)}, u32[]{:S(2)}, u32[]{:S(2)}) %collective-permute-start.4) | collective-permute-done | bytes 491552 | tf_op jit(solution)/shard_map/ppermute | solution.py:60
  287.7 13.5 %collective-permute-start.10 = (bf16[3,1,40,2048]{3,2,0,1:T(8,128)(2,1)S(1)}, bf16[3,1,40,2048]{3,2,0,1:T(8,128)(2,1)S(1)}, u32[]{:S(2)}, u32[]{:S(2)}) collective-permute-start(bf16[3,1,40,2048]{3,2,0,1:T(8,128)(2,1)S(1)} %bitcast.215), channel_id=1, source_target_pairs={{0,22},{2,24},{4,26},{6,28},{8,30},{10,0},{12,2},{14,4},{16,6},{18... | collective-permute-start | bytes 1474568 | tf_op jit(solution)/shard_map/ppermute | solution.py:60
  302.0 21.5 %collective-permute-start.11 = (bf16[3,1,40,2048]{3,2,0,1:T(8,128)(2,1)S(1)}, bf16[3,1,40,2048]{3,2,0,1:T(8,128)(2,1)S(1)}, u32[]{:S(2)}, u32[]{:S(2)}) collective-permute-start(bf16[3,1,40,2048]{3,2,0,1:T(8,128)(2,1)S(1)} %bitcast.214), channel_id=1, source_target_pairs={{0,24},{2,26},{4,28},{6,30},{8,0},{10,2},{12,4},{14,6},{16,8},{18,... | collective-permute-start | bytes 1474568 | tf_op jit(solution)/shard_map/ppermute | solution.py:60
  328.9 15.6 %collective-permute-start.13 = (bf16[3,1,40,2048]{3,2,0,1:T(8,128)(2,1)S(1)}, bf16[3,1,40,2048]{3,2,0,1:T(8,128)(2,1)S(1)}, u32[]{:S(2)}, u32[]{:S(2)}) collective-permute-start(bf16[3,1,40,2048]{3,2,0,1:T(8,128)(2,1)S(1)} %bitcast.212), channel_id=1, source_target_pairs={{0,28},{2,30},{4,0},{6,2},{8,4},{10,6},{12,8},{14,10},{16,12},{18,... | collective-permute-start | bytes 1474568 | tf_op jit(solution)/shard_map/ppermute | solution.py:60
  345.3 12.5 %collective-permute-start.14 = (bf16[3,1,40,2048]{3,2,0,1:T(8,128)(2,1)S(1)}, bf16[3,1,40,2048]{3,2,0,1:T(8,128)(2,1)S(1)}, u32[]{:S(2)}, u32[]{:S(2)}) collective-permute-start(bf16[3,1,40,2048]{3,2,0,1:T(8,128)(2,1)S(1)} %bitcast.211), channel_id=1, source_target_pairs={{0,30},{2,0},{4,2},{6,4},{8,6},{10,8},{12,10},{14,12},{16,14},{18,... | collective-permute-start | bytes 1474568 | tf_op jit(solution)/shard_map/ppermute | solution.py:60
  368.8 18.2 %gather_fusion.1 = bf16[16,3,40,2048]{3,2,1,0:T(8,128)(2,1)} fusion(bf16[16,3,40,2048]{3,2,1,0:T(8,128)(2,1)} %bitcast.39, s32[1024]{0:T(1024)S(1)} %pad_clamp_fusion), kind=kCustom, calls=%fused_computation.1 | custom fusion | bytes 15728704 | tf_op jit(solution)/shard_map/gather | solution.py:62
  391.3 25.3 %copy.101 = bf16[640,3,2048]{2,1,0:T(4,128)(2,1)} copy(bf16[640,3,2048]{2,0,1:T(8,128)(2,1)S(1)} %bitcast.173) | data formatting | bytes 15728640 | tf_op jit(solution)/shard_map/reshape;reshape | solution.py:41
  416.6 7.6 broadcast_in_dim.179
  424.2 85.1 %scatter_fusion = bf16[3,512,2048]{2,0,1:T(4,128)(2,1)} fusion(bf16[3,512,2048]{2,0,1:T(4,128)(2,1)} %broadcast_in_dim.179, s32[640]{0:T(1024)S(1)} %fusion.213, bf16[640,3,2048]{2,1,0:T(4,128)(2,1)} %copy.101), kind=kCustom, calls=%fused_computation.2 | custom fusion | bytes 23595520 | tf_op jit(solution)/shard_map/scatter | solution.py:44
  509.3 20.8 %fusion.234 = (bf16[1,512,2048]{2,0,1:T(2,128)(2,1)}, bf16[1,512,2048]{2,0,1:T(2,128)(2,1)}, bf16[1,512,2048]{2,0,1:T(2,128)(2,1)}) fusion(bf16[3,512,2048]{2,0,1:T(4,128)(2,1)} %scatter_fusion), kind=kLoop, calls=%fused_computation.356 | loop fusion | bytes 12582912 | tf_op jit(solution)/shard_map/slice | solution.py:75
  530.1 9.0 %copy.102 = bf16[1,512,2048]{1,2,0:T(8,128)(2,1)S(1)} copy(bf16[1,512,2048]{2,0,1:T(2,128)(2,1)} %get-tuple-element.146) | data formatting | bytes 4194304 | tf_op jit(solution)/shard_map/slice | solution.py:75
  539.0 10.5 %copy.103 = bf16[1,512,2048]{1,2,0:T(8,128)(2,1)} copy(bf16[1,512,2048]{2,0,1:T(2,128)(2,1)} %get-tuple-element.147) | data formatting | bytes 4194304 | tf_op jit(solution)/shard_map/slice | solution.py:75
  555.0 34.7 %all-reduce = f32[16]{0:T(128)S(1)} all-reduce(f32[16]{0:T(128)S(1)} %dynamic-update-slice), channel_id=1, replica_groups=mesh['seq'=16,'head'=2] {'seq'}, use_global_device_ids=true, to_apply=%add | all-reduce | flops 16 | bytes 128
  593.4 6.9 copy_bitcast_fusion
  600.3 81.7 %all-gather.3.cloned.1.call-done = f32[256,128,128]{2,1,0:T(8,128)} async-done(((f32[16,128,128]{2,1,0:T(8,128)}), f32[256,128,128]{2,1,0:T(8,128)}) %all-gather.3.cloned.1.call-update) | async-done | bytes 16777232 | tf_op jit(solution)/shard_map/all_gather | solution.py:23
  682.0 56.6 %while.14 = (s32[]{:T(128)}, f32[16,128,128]{2,1,0:T(8,128)S(1)}, s32[]{:T(128)}, f32[16,16,128,128]{3,2,1,0:T(8,128)}, f32[16]{0:T(128)S(1)}, /*index=5*/s32[]{:T(128)}, f32[1]{0:T(128)}, s32[]{:T(128)}) while((s32[]{:T(128)}, f32[16,128,128]{2,1,0:T(8,128)S(1)}, s32[]{:T(128)}, f32[16,16,128,128]{3,2,1,0:T(8,128)}, ...), condition=%wide.region_6.7_spmd.clone, body=%wide.region_5.6_spmd.clone.sunk | while | flops 1048581 | bytes 3145873 | solution.py:35
  (240 shorter events, 180.1 us)
Async XLA Ops:
  19.6 7.3 copy-start.28
  19.6 8.9 %copy-start.26 = (s32[1,16,40]{2,1,0:T(8,128)S(1)}, s32[1,16,40]{2,1,0:T(8,128)}, u32[]{:S(2)}) copy-start(s32[1,16,40]{2,1,0:T(8,128)} %param.9) | copy-start | bytes 7684
  19.6 9.0 %copy-start.25 = (s32[1,16,40]{2,1,0:T(8,128)S(1)}, s32[1,16,40]{2,1,0:T(8,128)}, u32[]{:S(2)}) copy-start(s32[1,16,40]{2,1,0:T(8,128)} %param.8) | copy-start | bytes 7684
  19.6 101.0 %all-to-all-start = ((bf16[3,256,4096]{1,0,2:T(4,128)(2,1)}), bf16[3,256,4096]{1,0,2:T(4,128)(2,1)}, u32[]{:S(2)}, u32[]{:S(2)}) async-start(bf16[3,256,4096]{1,0,2:T(4,128)(2,1)} %copy.80), calls=%async_computation | async-start | bytes 16777216 | tf_op jit(solution)/shard_map/all_to_all | solution.py:69
  26.7 655.3 %all-gather.3.cloned.1.call-start = ((), (), s32[]{:S(2)}) async-start(), calls=%async_computation.1 | async-start | bytes 17825792 | tf_op jit(solution)/shard_map/all_gather | solution.py:23
  186.4 14.2 %collective-permute-start = (bf16[3,1,40,2048]{3,2,0,1:T(8,128)(2,1)S(1)}, bf16[3,1,40,2048]{3,2,0,1:T(8,128)(2,1)S(1)}, u32[]{:S(2)}, u32[]{:S(2)}) collective-permute-start(bf16[3,1,40,2048]{3,2,0,1:T(8,128)(2,1)S(1)} %bitcast.224), channel_id=1, source_target_pairs={{0,2},{2,4},{4,6},{6,8},{8,10},{10,12},{12,14},{14,16},{16,18},{18... | collective-permute-start | bytes 1474568 | tf_op jit(solution)/shard_map/ppermute | solution.py:60
  188.0 17.0 %collective-permute-start.1 = (bf16[3,1,40,2048]{3,2,0,1:T(8,128)(2,1)S(1)}, bf16[3,1,40,2048]{3,2,0,1:T(8,128)(2,1)S(1)}, u32[]{:S(2)}, u32[]{:S(2)}) collective-permute-start(bf16[3,1,40,2048]{3,2,0,1:T(8,128)(2,1)S(1)} %bitcast.225), channel_id=1, source_target_pairs={{0,4},{2,6},{4,8},{6,10},{8,12},{10,14},{12,16},{14,18},{16,20},{1... | collective-permute-start | bytes 1474568 | tf_op jit(solution)/shard_map/ppermute | solution.py:60
  189.7 21.9 %collective-permute-start.2 = (bf16[3,1,40,2048]{3,2,0,1:T(8,128)(2,1)S(1)}, bf16[3,1,40,2048]{3,2,0,1:T(8,128)(2,1)S(1)}, u32[]{:S(2)}, u32[]{:S(2)}) collective-permute-start(bf16[3,1,40,2048]{3,2,0,1:T(8,128)(2,1)S(1)} %bitcast.222), channel_id=1, source_target_pairs={{0,6},{2,8},{4,10},{6,12},{8,14},{10,16},{12,18},{14,20},{16,22},{... | collective-permute-start | bytes 1474568 | tf_op jit(solution)/shard_map/ppermute | solution.py:60
  192.1 22.9 %collective-permute-start.3 = (bf16[3,1,40,2048]{3,2,0,1:T(8,128)(2,1)S(1)}, bf16[3,1,40,2048]{3,2,0,1:T(8,128)(2,1)S(1)}, u32[]{:S(2)}, u32[]{:S(2)}) collective-permute-start(bf16[3,1,40,2048]{3,2,0,1:T(8,128)(2,1)S(1)} %bitcast.220), channel_id=1, source_target_pairs={{0,8},{2,10},{4,12},{6,14},{8,16},{10,18},{12,20},{14,22},{16,24},... | collective-permute-start | bytes 1474568 | tf_op jit(solution)/shard_map/ppermute | solution.py:60
  193.7 93.2 %collective-permute-start.4 = (bf16[3,1,40,2048]{3,2,0,1:T(8,128)(2,1)S(1)}, bf16[3,1,40,2048]{3,2,0,1:T(8,128)(2,1)S(1)}, u32[]{:S(2)}, u32[]{:S(2)}) collective-permute-start(bf16[3,1,40,2048]{3,2,0,1:T(8,128)(2,1)S(1)} %bitcast.218), channel_id=1, source_target_pairs={{0,10},{2,12},{4,14},{6,16},{8,18},{10,20},{12,22},{14,24},{16,26}... | collective-permute-start | bytes 1474568 | tf_op jit(solution)/shard_map/ppermute | solution.py:60
  200.6 87.1 %collective-permute-start.5 = (bf16[3,1,40,2048]{3,2,0,1:T(8,128)(2,1)S(1)}, bf16[3,1,40,2048]{3,2,0,1:T(8,128)(2,1)S(1)}, u32[]{:S(2)}, u32[]{:S(2)}) collective-permute-start(bf16[3,1,40,2048]{3,2,0,1:T(8,128)(2,1)S(1)} %bitcast.223), channel_id=1, source_target_pairs={{0,12},{2,14},{4,16},{6,18},{8,20},{10,22},{12,24},{14,26},{16,28}... | collective-permute-start | bytes 1474568 | tf_op jit(solution)/shard_map/ppermute | solution.py:60
  205.0 97.0 %collective-permute-start.6 = (bf16[3,1,40,2048]{3,2,0,1:T(8,128)(2,1)S(1)}, bf16[3,1,40,2048]{3,2,0,1:T(8,128)(2,1)S(1)}, u32[]{:S(2)}, u32[]{:S(2)}) collective-permute-start(bf16[3,1,40,2048]{3,2,0,1:T(8,128)(2,1)S(1)} %bitcast.221), channel_id=1, source_target_pairs={{0,14},{2,16},{4,18},{6,20},{8,22},{10,24},{12,26},{14,28},{16,30}... | collective-permute-start | bytes 1474568 | tf_op jit(solution)/shard_map/ppermute | solution.py:60
  211.6 112.8 %collective-permute-start.7 = (bf16[3,1,40,2048]{3,2,0,1:T(8,128)(2,1)S(1)}, bf16[3,1,40,2048]{3,2,0,1:T(8,128)(2,1)S(1)}, u32[]{:S(2)}, u32[]{:S(2)}) collective-permute-start(bf16[3,1,40,2048]{3,2,0,1:T(8,128)(2,1)S(1)} %bitcast.219), channel_id=1, source_target_pairs={{0,16},{2,18},{4,20},{6,22},{8,24},{10,26},{12,28},{14,30},{16,0},... | collective-permute-start | bytes 1474568 | tf_op jit(solution)/shard_map/ppermute | solution.py:60
  215.0 113.9 %collective-permute-start.8 = (bf16[3,1,40,2048]{3,2,0,1:T(8,128)(2,1)S(1)}, bf16[3,1,40,2048]{3,2,0,1:T(8,128)(2,1)S(1)}, u32[]{:S(2)}, u32[]{:S(2)}) collective-permute-start(bf16[3,1,40,2048]{3,2,0,1:T(8,128)(2,1)S(1)} %bitcast.217), channel_id=1, source_target_pairs={{0,18},{2,20},{4,22},{6,24},{8,26},{10,28},{12,30},{14,0},{16,2},{... | collective-permute-start | bytes 1474568 | tf_op jit(solution)/shard_map/ppermute | solution.py:60
  286.9 58.5 %collective-permute-start.9 = (bf16[3,1,40,2048]{3,2,0,1:T(8,128)(2,1)S(1)}, bf16[3,1,40,2048]{3,2,0,1:T(8,128)(2,1)S(1)}, u32[]{:S(2)}, u32[]{:S(2)}) collective-permute-start(bf16[3,1,40,2048]{3,2,0,1:T(8,128)(2,1)S(1)} %bitcast.216), channel_id=1, source_target_pairs={{0,20},{2,22},{4,24},{6,26},{8,28},{10,30},{12,0},{14,2},{16,4},{1... | collective-permute-start | bytes 1474568 | tf_op jit(solution)/shard_map/ppermute | solution.py:60
  287.7 71.0 %collective-permute-start.10 = (bf16[3,1,40,2048]{3,2,0,1:T(8,128)(2,1)S(1)}, bf16[3,1,40,2048]{3,2,0,1:T(8,128)(2,1)S(1)}, u32[]{:S(2)}, u32[]{:S(2)}) collective-permute-start(bf16[3,1,40,2048]{3,2,0,1:T(8,128)(2,1)S(1)} %bitcast.215), channel_id=1, source_target_pairs={{0,22},{2,24},{4,26},{6,28},{8,30},{10,0},{12,2},{14,4},{16,6},{18... | collective-permute-start | bytes 1474568 | tf_op jit(solution)/shard_map/ppermute | solution.py:60
  302.0 57.5 %collective-permute-start.11 = (bf16[3,1,40,2048]{3,2,0,1:T(8,128)(2,1)S(1)}, bf16[3,1,40,2048]{3,2,0,1:T(8,128)(2,1)S(1)}, u32[]{:S(2)}, u32[]{:S(2)}) collective-permute-start(bf16[3,1,40,2048]{3,2,0,1:T(8,128)(2,1)S(1)} %bitcast.214), channel_id=1, source_target_pairs={{0,24},{2,26},{4,28},{6,30},{8,0},{10,2},{12,4},{14,6},{16,8},{18,... | collective-permute-start | bytes 1474568 | tf_op jit(solution)/shard_map/ppermute | solution.py:60
  324.4 36.0 %collective-permute-start.12 = (bf16[3,1,40,2048]{3,2,0,1:T(8,128)(2,1)S(1)}, bf16[3,1,40,2048]{3,2,0,1:T(8,128)(2,1)S(1)}, u32[]{:S(2)}, u32[]{:S(2)}) collective-permute-start(bf16[3,1,40,2048]{3,2,0,1:T(8,128)(2,1)S(1)} %bitcast.213), channel_id=1, source_target_pairs={{0,26},{2,28},{4,30},{6,0},{8,2},{10,4},{12,6},{14,8},{16,10},{18,... | collective-permute-start | bytes 1474568 | tf_op jit(solution)/shard_map/ppermute | solution.py:60
  328.9 34.0 %collective-permute-start.13 = (bf16[3,1,40,2048]{3,2,0,1:T(8,128)(2,1)S(1)}, bf16[3,1,40,2048]{3,2,0,1:T(8,128)(2,1)S(1)}, u32[]{:S(2)}, u32[]{:S(2)}) collective-permute-start(bf16[3,1,40,2048]{3,2,0,1:T(8,128)(2,1)S(1)} %bitcast.212), channel_id=1, source_target_pairs={{0,28},{2,30},{4,0},{6,2},{8,4},{10,6},{12,8},{14,10},{16,12},{18,... | collective-permute-start | bytes 1474568 | tf_op jit(solution)/shard_map/ppermute | solution.py:60
  345.3 22.7 %collective-permute-start.14 = (bf16[3,1,40,2048]{3,2,0,1:T(8,128)(2,1)S(1)}, bf16[3,1,40,2048]{3,2,0,1:T(8,128)(2,1)S(1)}, u32[]{:S(2)}, u32[]{:S(2)}) collective-permute-start(bf16[3,1,40,2048]{3,2,0,1:T(8,128)(2,1)S(1)} %bitcast.211), channel_id=1, source_target_pairs={{0,30},{2,0},{4,2},{6,4},{8,6},{10,8},{12,10},{14,12},{16,14},{18,... | collective-permute-start | bytes 1474568 | tf_op jit(solution)/shard_map/ppermute | solution.py:60
  549.5 40.2 %copy-start.27 = (f32[2048]{0:T(1024)S(1)}, f32[2048]{0:T(1024)}, u32[]{:S(2)}) copy-start(f32[2048]{0:T(1024)} %param.11) | copy-start | bytes 24580
  790.8 5.8 copy-start.4
  790.8 5.9 copy-start.3
  790.8 6.0 copy-start.2
  (23 other events, 98.6 us)
Sparse Core Ops, SparseCore 0:
  553.0 128.8 all-gather.2
